TPU v7x, 32 devices: a whole 2x2x4 slice. The times are simulated.
32 devices in a mesh: leaf: 32 (over z, y, x, core).
Axes of the slice: x: 2, y: 2, z: 4, core: 2. Of those that a mesh axis runs over, the one named last changes fastest.
Arguments:
- points: float32 [3, 131072], P(None, 'leaf'), may hold values from 0 to 1
- rhs: float32 [16, 131072], P(None, 'leaf'), may hold values from -6 to 6
- leaf_basis: float32 [32, 131072], P(None, 'leaf'), may hold values from -0.75 to 0.75
- transfer: float32 [32, 32, 2688], P(None, None, 'leaf'), may hold values from -0.5 to 0.5
- proxies: float32 [3, 32, 2720], P(None, None, 'leaf'), may hold values from 0 to 1
- near_list: int32 [2048, 5], P('leaf'), may hold values from -1 to 2047, as said below
- couple_list: int32 [2688, 20], P('leaf'), may hold values from -1 to 2047, as said below
- root_list: int32 [32, 32], P('leaf'), may hold values from -1 to 31, as said below
Outputs:
- product: float32 [16, 131072], P(None, 'leaf')
Inputs may be any that keep to these rules, and one draw needn't show every extreme that they name: `near_list`: entry [t, j] is the leaf t + j - 2 if the block of leaves t and t + j - 2 is near, else -1; every leaf is near itself. Nearness is defined level by level: at level 0 roots t and s are near when they differ by at most a per-root reach of 1 to 2 (the larger of the two); below, two clusters are near when their parents are near and they differ by at most the larger of their reaches. Near leaf blocks, with the coupled pairs of the other two lists, cover every pair of points exactly once. `couple_list`: the row of a cluster t of level l lists in slot j the cluster s = 4 * (t // 4 - 2) + j of level l if s exists, the parents of t and s are near and t and s are not near, else -1. `root_list`: entry [t, s] is s if roots t and s are not near, else -1.
All inputs are finite; a program needn't handle non-finite values.
Results may differ from a plain program's by a relative error of at most 0.0003.
Values sent between devices are 32-bit elements; how exact they have to be, the bound alone decides.
No kernel may reach another device: no remote copies, remote signals or barrier semaphores. Data moves between devices by JAX's collectives and lax.ppermute only.
A program may use at most 128 MiB of HBM per device.

v0:
```python
import math
import jax
import jax.numpy as jnp
from jax import lax
from jax.sharding import PartitionSpec as P

LEAF = 64
LEVELS = 3
REACH = 2
HALO = 11
LEAF_DEV = 64
kernel_band = 0.1
highest = lax.Precision.HIGHEST


def with_halo_2(cells, sides, width):
    for axis, dim in sides:
        count = lax.axis_size(axis)
        ends = count - 1
        head = lax.slice_in_dim(cells, 0, width, axis=dim)
        tail = lax.slice_in_dim(cells, cells.shape[dim] - width, cells.shape[dim], axis=dim)
        cells = jnp.concatenate(
            [
                lax.ppermute(tail, axis, [(i, (i + 1) % count) for i in range(ends)]),
                cells,
                lax.ppermute(head, axis, [((i + 1) % count, i) for i in range(ends)]),
            ],
            axis=dim,
        )
    return cells


def kernel_sq(left_pts, right_pts):
    length = (
        (left_pts[0] - right_pts[0]) ** 2
        + (left_pts[1] - right_pts[1]) ** 2
        + (left_pts[2] - right_pts[2]) ** 2
    )
    return jnp.exp(-length / kernel_band)


def by_blocks(method, inputs, length, stride, out_shape):
    stride = math.gcd(length, stride)

    def advance(step_no, accumulated):
        pieces = [operand for operand in inputs]
        return method(*pieces)

    return lax.fori_loop(0, length // stride, advance, jnp.zeros(out_shape, jnp.float32))


def couple(target_prox, lookup, source_prox, listed):
    usable = listed.T >= 0
    clipped = jnp.where(usable, listed.T, 0)

    def one_block(target_blk, clipped_blk, usable_blk):
        coeff_blk = jnp.take(lookup, clipped_blk, axis=2)
        prox_blk = jnp.take(source_prox, clipped_blk, axis=2)
        kernel = kernel_sq(
            target_blk[:, :, None, None, :], prox_blk[:, None, :, :, :]
        ) * usable_blk.astype(coeff_blk.dtype)
        return jnp.einsum("absn,bksn->akn", kernel, coeff_blk, precision=highest)

    extent = listed.shape[0]
    return by_blocks(
        one_block,
        [target_prox, clipped, usable],
        extent,
        128,
        (lookup.shape[0], lookup.shape[1], extent),
    )


def near_local(targets, lookup, listed, vectors):
    leaves = targets.shape[1]
    total = jnp.zeros((vectors, leaves, targets.shape[2]), jnp.float32)
    for slot_no in range(listed.shape[1]):
        window = lookup[:, slot_no : slot_no + leaves]
        usable = (listed[:, slot_no] >= 0).astype(jnp.float32)
        kernel = (
            kernel_sq(targets[:, :, :, None], window[vectors:, :, None, :]) * usable[:, None, None]
        )
        total = total + jnp.einsum("nij,knj->kni", kernel, window[:vectors], precision=highest)
    return total


def body(points, rhs, leaf_basis, transfer, proxies, near_list, couple_list, root_list):
    device = lax.axis_index("leaf")
    rank_dim = leaf_basis.shape[0]
    vectors = rhs.shape[0]
    leaves = LEAF_DEV
    basis_grid = leaf_basis.reshape(rank_dim, leaves, LEAF)
    coeffs = [None] * (LEVELS + 1)
    coeffs[LEVELS] = jnp.einsum(
        "rnp,knp->rkn", basis_grid, rhs.reshape(vectors, leaves, LEAF), precision=highest
    )
    level_prox = []
    mappings = [None]
    entries = [None]
    for level_no in range(LEVELS + 1):
        extent = 4**level_no
        begin_at = (extent - 1) // 3
        level_prox.append(proxies[:, :, begin_at : begin_at + extent])
        if level_no > 0:
            mappings.append(transfer[:, :, begin_at - 1 : begin_at - 1 + extent])
            entries.append(couple_list[begin_at - 1 : begin_at - 1 + extent])
    for level_no in range(LEVELS, 0, -1):
        merged = jnp.einsum("abn,akn->bkn", mappings[level_no], coeffs[level_no], precision=highest)
        coeffs[level_no - 1] = merged.reshape(rank_dim, vectors, -1, 4).sum(axis=3)
    top_count = 3
    stacked_coeffs = jnp.concatenate([coeffs[level_no] for level_no in range(top_count)], axis=2)
    stacked_prox = jnp.concatenate(level_prox[:top_count], axis=2)
    gathered_coeffs, gathered_prox = (
        lax.all_gather(stacked_coeffs, "leaf", axis=2, tiled=True),
        lax.all_gather(stacked_prox, "leaf", axis=2, tiled=True),
    )
    group = stacked_coeffs.shape[2]
    roots = gathered_coeffs.shape[2] // group
    gathered_coeffs = gathered_coeffs.reshape(rank_dim, vectors, roots, group)
    gathered_prox = gathered_prox.reshape(3, rank_dim, roots, group)
    coupled = []
    for level_no in range(LEVELS + 1):
        extent = 4**level_no
        if level_no < top_count:
            begin_at = (extent - 1) // 3
            lookup = gathered_coeffs[:, :, :, begin_at : begin_at + extent].reshape(
                rank_dim, vectors, roots * extent
            )
            source_prox = gathered_prox[:, :, :, begin_at : begin_at + extent].reshape(
                3, rank_dim, roots * extent
            )
            listed = root_list if level_no == 0 else entries[level_no]
        else:
            joined = jnp.concatenate(
                [
                    coeffs[level_no].reshape(rank_dim * vectors, extent),
                    level_prox[level_no].reshape(3 * rank_dim, extent),
                ],
                axis=0,
            )
            with_rim = with_halo_2(joined, (("leaf", 1),), HALO)
            width_rim = with_rim.shape[1]
            lookup = with_rim[: rank_dim * vectors].reshape(rank_dim, vectors, width_rim)
            source_prox = with_rim[rank_dim * vectors :].reshape(3, rank_dim, width_rim)
            base_index = device * extent - HALO
            listed = jnp.where(entries[level_no] >= 0, entries[level_no] - base_index, -1)
        coupled.append(couple(level_prox[level_no], lookup, source_prox, listed))
    downward = coupled[0]
    for level_no in range(1, LEVELS + 1):
        downward = coupled[level_no] + jnp.einsum(
            "abn,bkn->akn", mappings[level_no], jnp.repeat(downward, 4, axis=2), precision=highest
        )
    joined_pts = jnp.concatenate([rhs, points], axis=0)
    with_halo = with_halo_2(joined_pts, (("leaf", 1),), REACH * LEAF)
    lookup_pts = with_halo.reshape(vectors + 3, leaves + 2 * REACH, LEAF)
    targets = points.reshape(3, leaves, LEAF)
    near_part = near_local(targets, lookup_pts, near_list, vectors)
    far_part = jnp.einsum("rnp,rkn->knp", basis_grid, downward, precision=highest)
    return (near_part + far_part).reshape(vectors, leaves * LEAF)


def solution(mesh):
    in_specs = (
        P(None, "leaf"),
        P(None, "leaf"),
        P(None, "leaf"),
        P(None, None, "leaf"),
        P(None, None, "leaf"),
        P("leaf", None),
        P("leaf", None),
        P("leaf", None),
    )
    out_specs = P(None, "leaf")
    return jax.shard_map(body, mesh=mesh, in_specs=in_specs, out_specs=out_specs, check_vma=False)
```

profile of v0, /device:TPU:0, one launch (start us, length us, event | category | flops | bytes accessed | tf_op | source)
XLA Modules:
  0.0 221.3 jit_solution(3418273684707584734)
XLA Ops:
  7.9 2.0 slice.388
  12.4 1.7 copy.166
  14.4 3.6 %convolution_bitcast_fusion = f32[32,16,64]{0,1,2:T(8,128)S(1)} fusion(f32[32,64,64]{2,1,0:T(8,128)S(1)} %reshape.364, f32[16,64,64]{2,1,0:T(8,128)} %reshape.363), kind=kOutput, calls=%fused_computation.140 | convolution fusion | flops 25165824 | bytes 917504 | tf_op jit(solution)/shard_map/rnp,knp->rkn/dot_general | solution.py:94
  21.8 2.4 %collective-permute-start.2 = (f32[608,11]{1,0:T(8,128)}, f32[608,11]{1,0:T(8,128)S(1)}, u32[]{:S(2)}, u32[]{:S(2)}) collective-permute-start(f32[608,11]{1,0:T(8,128)} %get-tuple-element.121), channel_id=1, source_target_pairs={{0,1},{1,2},{2,3},{3,4},{4,5},{5,6},{6,7},{7,8},{8,9},{9,10},{10,1... | collective-permute-start | bytes 80264 | tf_op jit(solution)/shard_map/ppermute | solution.py:24
  26.2 5.7 %collective-permute-start = (f32[19,128]{1,0:T(8,128)}, f32[19,128]{1,0:T(8,128)}, u32[]{:S(2)}, u32[]{:S(2)}) collective-permute-start(f32[19,128]{1,0:T(8,128)} %get-tuple-element.119), channel_id=1, source_target_pairs={{0,1},{1,2},{2,3},{3,4},{4,5},{5,6},{6,7},{7,8},{8,9},{9,10},{10,1... | collective-permute-start | bytes 29192 | tf_op jit(solution)/shard_map/ppermute | solution.py:24
  34.7 50.4 %all_gather.7 = f32[3,32,672]{1,0,2:T(4,128)S(1)} all-gather(f32[3,32,21]{1,0,2:T(4,128)S(1)} %copy.169), channel_id=1, replica_groups=mesh['leaf'=32] {'leaf'}, dimensions={2}, use_global_device_ids=true | all-gather | bytes 266112 | tf_op jit(solution)/shard_map/all_gather | solution.py:115
  93.2 2.2 gather_fusion.3
  104.8 6.1 %fusion.87 = f32[64,16,64]{2,1,0:T(8,128)S(1)} fusion(f32[64]{0:T(128)S(1)} %get-tuple-element.145, f32[64,64]{1,0:T(8,128)S(1)} %get-tuple-element.100, f32[64,64]{1,0:T(8,128)S(1)} %get-tuple-element.101, f32[64,64]{1,0:T(8,128)S(1)} %get-tuple-element.102, f32[64,64]{1,0:T(8,128)S(1)} %sub.523, f32[64,64]{1,0:T(8,128)S(1)} %sub.518, ...), kind=kOutput, calls=%fused_computation.95 | convolution fusion | flops 53215232 | bytes 622848 | tf_op jit(solution)/shard_map/nij,knj->kni/dot_general | solution.py:83
  110.9 6.1 %fusion.74 = f32[64,16,64]{2,1,0:T(8,128)S(1)} fusion(f32[64]{0:T(128)S(1)} %get-tuple-element.144, f32[64,64]{1,0:T(8,128)S(1)} %get-tuple-element.89, f32[64,64]{1,0:T(8,128)S(1)} %get-tuple-element.90, f32[64,64]{1,0:T(8,128)S(1)} %get-tuple-element.98, f32[64,64]{1,0:T(8,128)S(1)} %sub.523, f32[64,64]{1,0:T(8,128)S(1)} %sub.518, ...), kind=kOutput, calls=%fused_computation.82 | convolution fusion | flops 53215232 | bytes 622848 | tf_op jit(solution)/shard_map/nij,knj->kni/dot_general | solution.py:83
  117.0 6.1 %fusion.48 = f32[64,16,64]{2,1,0:T(8,128)S(1)} fusion(f32[64]{0:T(128)S(1)} %get-tuple-element.147, f32[64,64]{1,0:T(8,128)S(1)} %get-tuple-element.103, f32[64,64]{1,0:T(8,128)S(1)} %get-tuple-element.99, f32[64,64]{1,0:T(8,128)S(1)} %get-tuple-element.88, f32[64,64]{1,0:T(8,128)S(1)} %sub.523, f32[64,64]{1,0:T(8,128)S(1)} %sub.518, ...), kind=kOutput, calls=%fused_computation.56 | convolution fusion | flops 53215232 | bytes 622848 | tf_op jit(solution)/shard_map/nij,knj->kni/dot_general | solution.py:83
  123.0 6.1 %fusion.138 = f32[64,16,64]{2,1,0:T(8,128)S(1)} fusion(f32[64,16,64]{2,1,0:T(8,128)S(1)} %fusion.74, f32[64,16,64]{2,1,0:T(8,128)S(1)} %fusion.87, f32[64]{0:T(128)S(1)} %get-tuple-element.146, f32[64,64]{1,0:T(8,128)S(1)} %get-tuple-element.104, f32[64,64]{1,0:T(8,128)S(1)} %sub.523, f32[64,64]{1,0:T(8,128)S(1)} %get-tuple-element.112, ...), kind=kOutput, calls=%fused_computation.143 | convolution fusion | flops 53346304 | bytes 1147136 | tf_op jit(solution)/shard_map/nij,knj->kni/dot_general | solution.py:83
  129.1 6.0 %fusion.144 = f32[64,16,64]{2,1,0:T(8,128)} fusion(f32[64,16,64]{2,1,0:T(8,128)S(1)} %fusion.48, f32[64,16,64]{2,1,0:T(8,128)S(1)} %fusion.138, f32[64]{0:T(128)S(1)} %get-tuple-element.143, f32[64,64]{1,0:T(8,128)S(1)} %get-tuple-element.86, f32[64,64]{1,0:T(8,128)S(1)} %get-tuple-element.87, f32[64,64]{1,0:T(8,128)S(1)} %get-tuple-element.85, ...), kind=kOutput, calls=%fused_computation.145 | convolution fusion | flops 53346304 | bytes 1147136 | tf_op jit(solution)/shard_map/nij,knj->kni/dot_general | solution.py:83
  136.1 4.3 %gather_fusion.1 = f32[1280,3,32]{2,1,0:T(4,128)S(1)} fusion(f32[3,32,86]{1,0,2:T(4,128)S(1)} %copy.122, s32[2048]{0:T(1024)S(1)} %pad_clamp_fusion), kind=kCustom, calls=%fused_computation.1 | custom fusion | bytes 988160 | tf_op jit(solution)/shard_map/while/body/eval_jaxpr/jit(_take)/gather | solution.py:58
  140.4 2.6 %copy.154 = f32[20,64,3,32]{1,0,3,2:T(8,128)} copy(f32[20,64,3,32]{3,2,1,0:T(4,128)S(1)} %bitcast.205) | data formatting | bytes 983040 | tf_op jit(solution)/shard_map/while/body/eval_jaxpr/jit(_take)/gather | solution.py:58
  143.0 1.4 select_bitcast_fusion
  147.7 5.5 %gather_fusion = f32[1280,32,16]{1,2,0:T(8,128)} fusion(f32[32,16,86]{0,1,2:T(8,128)S(1)} %copy.120, s32[2048]{0:T(1024)S(1)} %pad_clamp_fusion), kind=kCustom, calls=%fused_computation | custom fusion | bytes 5248000 | tf_op jit(solution)/shard_map/while/body/eval_jaxpr/jit(_take)/gather | solution.py:57
  153.2 31.3 %fusion.130 = f32[64,16,32]{2,1,0:T(8,128)} fusion(f32[20,64]{1,0:T(8,128)S(1)} %copy-done.44, f32[32,20,64]{0,2,1:T(8,128)S(1)} %copy-done.15, f32[32,64]{0,1:T(8,128)S(1)} %copy-done.39, f32[32,20,64]{0,2,1:T(8,128)S(1)} %copy-done.14, f32[32,64]{0,1:T(8,128)S(1)} %copy-done.38, f32[32,20,64]{0,2,1:T(8,128)S(1)} %copy.124, f32[32,64]{0,1:T(8,128)S(1)} %copy-done.37, ...), kind=kOutput, calls=%fused_computation.141 | convolution fusion | flops 266731520 | bytes 3275008 | tf_op jit(solution)/shard_map/while/body/eval_jaxpr/absn,bksn->akn/dot_general | solution.py:62
  186.8 4.6 %slice.460 = f32[32,16,32,16]{0,1,3,2:T(8,128)} slice(f32[32,16,32,21]{0,1,3,2:T(8,128)} %bitcast.208), slice={[0:32], [0:16], [0:32], [5:21]} | slice | bytes 2097152 | tf_op jit(solution)/shard_map/slice | solution.py:126
  192.1 1.4 gather_fusion.6
  193.5 3.0 %gather_fusion.2 = f32[320,32,16]{1,2,0:T(8,128)S(1)} fusion(f32[32,16,512]{0,1,2:T(8,128)} %bitcast.203, s32[1024]{0:T(1024)S(1)} %get-tuple-element.151), kind=kCustom, calls=%fused_computation.2 | custom fusion | bytes 1312000 | tf_op jit(solution)/shard_map/while/body/eval_jaxpr/jit(_take)/gather | solution.py:57
  196.7 3.1 %fusion.153 = f32[4,16,32]{2,1,0:T(8,128)S(1)} fusion(f32[20,4,32,16]{2,3,1,0:T(8,128)S(1)} %bitcast.201, f32[20,4]{1,0:T(8,128)} %get-tuple-element.139, f32[32,20,4]{0,2,1:T(4,128)} %get-tuple-element.124, f32[32,4]{0,1:T(4,128)} %bitcast.234, f32[32,20,4]{0,2,1:T(4,128)} %get-tuple-element.125, f32[32,4]{0,1:T(4,128)} %bitcast.233, ...), kind=kOutput, calls=%fused_computation.150 | convolution fusion | flops 16670720 | bytes 204688 | tf_op jit(solution)/shard_map/while/body/eval_jaxpr/absn,bksn->akn/dot_general | solution.py:62
  201.1 8.3 %fusion.148 = f32[16,16,32]{2,1,0:T(8,128)S(1)} fusion(f32[20,16]{1,0:T(8,128)S(1)} %copy-done.43, f32[32,20,16]{0,2,1:T(8,128)S(1)} %copy-done.25, f32[32,16]{0,1:T(8,128)S(1)} %copy-done.47, f32[32,20,16]{0,2,1:T(8,128)S(1)} %copy-done.26, f32[32,16]{0,1:T(8,128)S(1)} %copy-done.46, f32[32,20,16]{0,2,1:T(8,128)S(1)} %copy-done.24, ...), kind=kOutput, calls=%fused_computation.149 | convolution fusion | flops 66682880 | bytes 818752 | tf_op jit(solution)/shard_map/while/body/eval_jaxpr/absn,bksn->akn/dot_general | solution.py:62
  210.0 1.7 fusion.129
  211.8 1.6 fusion.128
  (210 shorter events, 39.7 us)
Async XLA Ops:
  6.5 178.0 %all-gather.2.cloned.1.call-start = ((), (), s32[]{:S(2)}) async-start(), calls=%async_computation | async-start | bytes 5677056 | tf_op jit(solution)/shard_map/all_gather | solution.py:114
  10.3 7.7 %copy-start = (f32[32,64,64]{2,1,0:T(8,128)}, f32[32,64,64]{2,1,0:T(8,128)S(1)}, u32[]{:S(2)}) copy-start(f32[32,64,64]{2,1,0:T(8,128)S(1)} %reshape.364) | copy-start | bytes 1572868
  12.4 6.7 %copy-start.2 = (f32[32,32,64]{1,0,2:T(8,128)}, f32[32,32,64]{1,0,2:T(8,128)S(1)}, u32[]{:S(2)}) copy-start(f32[32,32,64]{1,0,2:T(8,128)S(1)} %copy.165) | copy-start | bytes 786436
  19.1 6.4 %copy-start.11 = (f32[16,4096]{1,0:T(8,128)S(1)}, f32[16,4096]{1,0:T(8,128)}, u32[]{:S(2)}) copy-start(f32[16,4096]{1,0:T(8,128)} %param.9) | copy-start | bytes 786436
  19.1 6.4 %copy-start.23 = (f32[3,4096]{1,0:T(4,128)S(1)}, f32[3,4096]{1,0:T(4,128)}, u32[]{:S(2)}) copy-start(f32[3,4096]{1,0:T(4,128)} %param.8) | copy-start | bytes 147460
  19.1 14.1 %copy-start.21 = (s32[84,20]{0,1:T(8,128)S(1)}, s32[84,20]{0,1:T(8,128)}, u32[]{:S(2)}) copy-start(s32[84,20]{0,1:T(8,128)} %param.14) | copy-start | bytes 20164
  20.8 64.3 %copy-start.55 = (s32[1,32]{1,0:T(1,128)S(1)}, s32[1,32]{1,0:T(1,128)}, u32[]{:S(2)}) copy-start(s32[1,32]{1,0:T(1,128)} %param.15) | copy-start | bytes 388
  20.9 114.2 %copy-start.12 = (f32[3,32,64]{2,1,0:T(8,128)}, f32[3,32,64]{2,1,0:T(8,128)S(1)}, u32[]{:S(2)}) copy-start(f32[3,32,64]{2,1,0:T(8,128)S(1)} %slice.375) | copy-start | bytes 73732
  21.8 113.3 %collective-permute-start.2 = (f32[608,11]{1,0:T(8,128)}, f32[608,11]{1,0:T(8,128)S(1)}, u32[]{:S(2)}, u32[]{:S(2)}) collective-permute-start(f32[608,11]{1,0:T(8,128)} %get-tuple-element.121), channel_id=1, source_target_pairs={{0,1},{1,2},{2,3},{3,4},{4,5},{5,6},{6,7},{7,8},{8,9},{9,10},{10,1... | collective-permute-start | bytes 80264 | tf_op jit(solution)/shard_map/ppermute | solution.py:24
  24.2 110.9 %collective-permute-start.3 = (f32[608,11]{1,0:T(8,128)}, f32[608,11]{1,0:T(8,128)S(1)}, u32[]{:S(2)}, u32[]{:S(2)}) collective-permute-start(f32[608,11]{1,0:T(8,128)} %get-tuple-element.122), channel_id=1, source_target_pairs={{1,0},{2,1},{3,2},{4,3},{5,4},{6,5},{7,6},{8,7},{9,8},{10,9},{11,1... | collective-permute-start | bytes 80264 | tf_op jit(solution)/shard_map/ppermute | solution.py:26
  26.2 77.3 %collective-permute-start = (f32[19,128]{1,0:T(8,128)}, f32[19,128]{1,0:T(8,128)}, u32[]{:S(2)}, u32[]{:S(2)}) collective-permute-start(f32[19,128]{1,0:T(8,128)} %get-tuple-element.119), channel_id=1, source_target_pairs={{0,1},{1,2},{2,3},{3,4},{4,5},{5,6},{6,7},{7,8},{8,9},{9,10},{10,1... | collective-permute-start | bytes 29192 | tf_op jit(solution)/shard_map/ppermute | solution.py:24
  31.9 71.6 %collective-permute-start.1 = (f32[19,128]{1,0:T(8,128)}, f32[19,128]{1,0:T(8,128)}, u32[]{:S(2)}, u32[]{:S(2)}) collective-permute-start(f32[19,128]{1,0:T(8,128)} %get-tuple-element.120), channel_id=1, source_target_pairs={{1,0},{2,1},{3,2},{4,3},{5,4},{6,5},{7,6},{8,7},{9,8},{10,9},{11,1... | collective-permute-start | bytes 29192 | tf_op jit(solution)/shard_map/ppermute | solution.py:26
  85.7 6.2 %copy-start.50 = (pred[32]{0:T(512)(128)(4,1)}, pred[32]{0:T(512)(128)(4,1)S(1)}, u32[]{:S(2)}) copy-start(pred[32]{0:T(512)(128)(4,1)S(1)} %get-tuple-element.148) | copy-start | bytes 100
  95.5 5.7 %copy-start.30 = (f32[32,64]{1,0:T(8,128)S(1)}, f32[32,64]{1,0:T(8,128)}, u32[]{:S(2)}) copy-start(f32[32,64]{1,0:T(8,128)} %get-tuple-element.135) | copy-start | bytes 24580
  95.5 6.4 %copy-start.29 = (f32[32,64]{1,0:T(8,128)S(1)}, f32[32,64]{1,0:T(8,128)}, u32[]{:S(2)}) copy-start(f32[32,64]{1,0:T(8,128)} %get-tuple-element.137) | copy-start | bytes 24580
  95.5 7.1 %copy-start.28 = (f32[32,64]{1,0:T(8,128)S(1)}, f32[32,64]{1,0:T(8,128)}, u32[]{:S(2)}) copy-start(f32[32,64]{1,0:T(8,128)} %get-tuple-element.136) | copy-start | bytes 24580
  95.5 7.8 %copy-start.27 = (f32[4096]{0:T(1024)S(1)}, f32[4096]{0:T(1024)}, u32[]{:S(2)}) copy-start(f32[4096]{0:T(1024)} %get-tuple-element.48) | copy-start | bytes 49156
  147.6 5.6 %copy-start.14 = (f32[32,20,64]{0,2,1:T(8,128)S(1)}, f32[32,20,64]{0,2,1:T(8,128)}, u32[]{:S(2)}) copy-start(f32[32,20,64]{0,2,1:T(8,128)} %copy.126) | copy-start | bytes 491524
  147.6 5.6 %copy-start.15 = (f32[32,20,64]{0,2,1:T(8,128)S(1)}, f32[32,20,64]{0,2,1:T(8,128)}, u32[]{:S(2)}) copy-start(f32[32,20,64]{0,2,1:T(8,128)} %copy.128) | copy-start | bytes 491524
  147.6 5.6 %copy-start.37 = (f32[32,64]{0,1:T(8,128)S(1)}, f32[32,64]{0,1:T(8,128)}, u32[]{:S(2)}) copy-start(f32[32,64]{0,1:T(8,128)} %copy.121) | copy-start | bytes 24580
  147.6 5.6 %copy-start.38 = (f32[32,64]{0,1:T(8,128)S(1)}, f32[32,64]{0,1:T(8,128)}, u32[]{:S(2)}) copy-start(f32[32,64]{0,1:T(8,128)} %copy.125) | copy-start | bytes 24580
  147.7 5.6 %copy-start.39 = (f32[32,64]{0,1:T(8,128)S(1)}, f32[32,64]{0,1:T(8,128)}, u32[]{:S(2)}) copy-start(f32[32,64]{0,1:T(8,128)} %copy.127) | copy-start | bytes 24580
  201.1 8.9 %copy-start.3 = (f32[32,32,64]{1,0,2:T(8,128)S(1)}, f32[32,32,64]{1,0,2:T(8,128)}, u32[]{:S(2)}) copy-start(f32[32,32,64]{1,0,2:T(8,128)} %copy-done.2) | copy-start | bytes 786436
  201.1 8.9 %copy-start.20 = (f32[64,16,32]{2,1,0:T(8,128)S(1)}, f32[64,16,32]{2,1,0:T(8,128)}, u32[]{:S(2)}) copy-start(f32[64,16,32]{2,1,0:T(8,128)} %fusion.130) | copy-start | bytes 393220
  (38 other events, 129.7 us)
Sparse Core Ops, SparseCore 0:
  20.6 72.6 all-gather.1
where the time goes:
time: 222 us; the launch traced here: 221 us
  matrix products  83.1 us (37%)
  local copies, waits for them, and re-layouts  55.7 us (25%)
  blocking collectives  50.4 us (23%)
  between operations  14.5 us (7%)
  starting transfers between devices  10.7 us (5%)
  other arithmetic  6.98 us (3%)
    all_gather x1, blocking collectives, body(): lax.all_gather(stacked_prox, 'leaf', axis=2, tiled=True)  50.4 us
    dot_general x4, matrix products, one_block(): return jnp.einsum('absn,bksn->akn', kernel, coeff_blk, precision=highest)  43.6 us
    dot_general x5, matrix products, near_local(): jnp.einsum('nij,knj->kni', kernel, window[:vectors], precision=highest)  30.2 us
    gather x4, local copies, waits for them, and re-layouts, one_block(): coeff_blk = jnp.take(lookup, clipped_blk, axis=2)  10.6 us
    gather x7, local copies, waits for them, and re-layouts, one_block(): prox_blk = jnp.take(source_prox, clipped_blk, axis=2)  10.4 us
    ppermute x2, starting transfers between devices, with_halo_2(): lax.ppermute(tail, axis, [(i, (i + 1) % count) for i in range(ends)])  8.1 us
    slice x2, local copies, waits for them, and re-layouts, body(): gathered_coeffs[:, :, :, begin_at:begin_at + extent]  5.94 us
    sub x10, local copies, waits for them, and re-layouts, kernel_sq(): left_pts[0] - right_pts[0]  4.64 us
  transfers between devices with their start and end apart: 5, of which 0 were waited for; matrix products, arithmetic and copies ran while one was open for 46% of the time, Pallas kernels for 0%

commit v1 on v0

--- a/solution.py
+++ b/solution.py
@@ -1,3 +1,4 @@
+import functools
 import math
 import jax
 import jax.numpy as jnp
@@ -11,6 +12,24 @@
 LEAF_DEV = 64
 kernel_band = 0.1
 highest = lax.Precision.HIGHEST
+
+
+def prepare_limits(here_x, axis_key):
+    kept_arr = lax.axis_size(axis_key)
+    d_next = lax.axis_index(axis_key)
+    last, val, all_rows = (kept_arr, d_next, here_x.shape[2])
+    heard, arr_now = (here_x, 1)
+    while arr_now < last:
+        outer = lax.ppermute(
+            heard, axis_key, [(dev_j, (dev_j - arr_now) % last) for dev_j in range(last)]
+        )
+        heard = jnp.concatenate([heard, outer], 2)
+        arr_now = 2 * arr_now
+    current_block = jnp.roll(heard, val * all_rows, 2)
+    return current_block
+
+
+enter_stages_all = functools.partial(prepare_limits, axis_key="leaf")
 
 
 def with_halo_2(cells, sides, width):
@@ -112,7 +131,7 @@
     stacked_prox = jnp.concatenate(level_prox[:top_count], axis=2)
     gathered_coeffs, gathered_prox = (
         lax.all_gather(stacked_coeffs, "leaf", axis=2, tiled=True),
-        lax.all_gather(stacked_prox, "leaf", axis=2, tiled=True),
+        enter_stages_all(stacked_prox),
     )
     group = stacked_coeffs.shape[2]
     roots = gathered_coeffs.shape[2] // group

time: 222 us -> 195 us (0.88)
  blocking collectives: 50.4 us -> 0 us
  starting transfers between devices: 10.7 us -> 21.8 us
  local copies, waits for them, and re-layouts: 55.7 us -> 65.2 us
    all_gather x1 -> x0, blocking collectives: 50.4 us -> none  [body(): lax.all_gather(stacked_prox, 'leaf', axis=2, tiled=True)]
    ppermute x0 -> x5, starting transfers between devices: none -> 14.9 us  [prepare_limits(): lax.ppermute(heard, axis_key, [(dev_j, (dev_j - arr_now) % last) for dev_...]
    slice x4, local copies, waits for them, and re-layouts: 0.44 us -> 4.81 us  [body(): gathered_prox[:, :, :, begin_at:begin_at + extent]]
    ppermute x2, starting transfers between devices: 8.1 us -> 4.33 us  [with_halo_2(): lax.ppermute(tail, axis, [(i, (i + 1) % count) for i in range(ends)])]
    reshape x3, local copies, waits for them, and re-layouts: 0.69 us -> 3.2 us  [body(): gathered_prox[:, :, :, begin_at:begin_at + extent]]
  transfers between devices with their start and end apart: 5 -> 10, of which waited for: 0 -> 0; matrix products, arithmetic and copies ran while one was open for 46% -> 66% of each run, Pallas kernels for 0% -> 0%
where the time goes in v1:
time: 195 us; the launch traced here: 194 us
  matrix products  83.2 us (43%)
  local copies, waits for them, and re-layouts  65.2 us (33%)
  starting transfers between devices  21.8 us (11%)
  between operations  14.6 us (7%)
  other arithmetic  9.18 us (5%)
    dot_general x4, matrix products, one_block(): return jnp.einsum('absn,bksn->akn', kernel, coeff_blk, precision=highest)  43.6 us
    dot_general x5, matrix products, near_local(): jnp.einsum('nij,knj->kni', kernel, window[:vectors], precision=highest)  30.2 us
    ppermute x5, starting transfers between devices, prepare_limits(): lax.ppermute(heard, axis_key, [(dev_j, (dev_j - arr_now) % last) for dev_...  14.9 us
    gather x7, local copies, waits for them, and re-layouts, one_block(): prox_blk = jnp.take(source_prox, clipped_blk, axis=2)  10.5 us
    gather x4, local copies, waits for them, and re-layouts, one_block(): coeff_blk = jnp.take(lookup, clipped_blk, axis=2)  9.89 us
    slice x2, local copies, waits for them, and re-layouts, body(): gathered_coeffs[:, :, :, begin_at:begin_at + extent]  5.94 us
    slice x4, local copies, waits for them, and re-layouts, body(): gathered_prox[:, :, :, begin_at:begin_at + extent]  4.81 us
    ppermute x2, starting transfers between devices, with_halo_2(): lax.ppermute(tail, axis, [(i, (i + 1) % count) for i in range(ends)])  4.33 us
  transfers between devices with their start and end apart: 10, of which 0 were waited for; matrix products, arithmetic and copies ran while one was open for 66% of the time, Pallas kernels for 0%

profile of v1, /device:TPU:0, one launch (start us, length us, event | category | flops | bytes accessed | tf_op | source)
XLA Modules:
  0.0 194.0 jit_solution(14367985823129712616)
XLA Ops:
  6.5 6.4 %collective-permute-start.4 = (f32[3,32,21]{2,1,0:T(8,128)}, f32[3,32,21]{2,1,0:T(8,128)S(1)}, u32[]{:S(2)}, u32[]{:S(2)}) collective-permute-start(f32[3,32,21]{2,1,0:T(8,128)} %bitcast.203), channel_id=1, source_target_pairs={{0,31},{1,0},{2,1},{3,2},{4,3},{5,4},{6,5},{7,6},{8,7},{9,8},{10,9... | collective-permute-start | bytes 24200 | tf_op jit(solution)/shard_map/ppermute | solution.py:23
  14.2 2.1 %slice.394 = f32[32,32,16]{2,1,0:T(8,128)} slice(f32[32,32,84]{2,1,0:T(8,128)} %param.11), slice={[0:32], [0:32], [4:20]} | slice | bytes 131072 | tf_op jit(solution)/shard_map/slice | solution.py:124
  20.8 3.6 %convolution_bitcast_fusion = f32[32,16,64]{0,1,2:T(8,128)S(1)} fusion(f32[32,64,64]{2,1,0:T(8,128)S(1)} %reshape.364, f32[16,64,64]{2,1,0:T(8,128)} %reshape.363), kind=kOutput, calls=%fused_computation.140 | convolution fusion | flops 25165824 | bytes 917504 | tf_op jit(solution)/shard_map/rnp,knp->rkn/dot_general | solution.py:113
  30.9 3.0 %collective-permute-start = (f32[19,128]{1,0:T(8,128)S(1)}, f32[19,128]{1,0:T(8,128)S(1)}, u32[]{:S(2)}, u32[]{:S(2)}) collective-permute-start(f32[19,128]{1,0:T(8,128)S(1)} %get-tuple-element.119), channel_id=1, source_target_pairs={{0,1},{1,2},{2,3},{3,4},{4,5},{5,6},{6,7},{7,8},{8,9},{9,10},{10,1... | collective-permute-start | bytes 29192 | tf_op jit(solution)/shard_map/ppermute | solution.py:43
  48.6 4.9 %collective-permute-start.5 = (f32[3,32,42]{2,1,0:T(8,128)S(1)}, f32[3,32,42]{2,1,0:T(8,128)S(1)}, u32[]{:S(2)}, u32[]{:S(2)}) collective-permute-start(f32[3,32,42]{2,1,0:T(8,128)S(1)} %pad_maximum_fusion.6), channel_id=1, source_target_pairs={{0,30},{1,31},{2,0},{3,1},{4,2},{5,3},{6,4},{7,5},{8,6},{9,7},{10,... | collective-permute-start | bytes 48392 | tf_op jit(solution)/shard_map/ppermute | solution.py:23
  54.6 6.0 %fusion.87 = f32[64,16,64]{2,1,0:T(8,128)S(1)} fusion(f32[64]{0:T(128)S(1)} %get-tuple-element.145, f32[64,64]{1,0:T(8,128)S(1)} %get-tuple-element.100, f32[64,64]{1,0:T(8,128)S(1)} %get-tuple-element.101, f32[64,64]{1,0:T(8,128)S(1)} %get-tuple-element.102, f32[64,64]{1,0:T(8,128)S(1)} %copy-done.33, f32[64,64]{1,0:T(8,128)S(1)} %copy-done.32, ...), kind=kOutput, calls=%fused_computation.95 | convolution fusion | flops 53215232 | bytes 622848 | tf_op jit(solution)/shard_map/nij,knj->kni/dot_general | solution.py:102
  60.6 6.1 %fusion.74 = f32[64,16,64]{2,1,0:T(8,128)S(1)} fusion(f32[64]{0:T(128)S(1)} %get-tuple-element.144, f32[64,64]{1,0:T(8,128)S(1)} %get-tuple-element.89, f32[64,64]{1,0:T(8,128)S(1)} %get-tuple-element.90, f32[64,64]{1,0:T(8,128)S(1)} %get-tuple-element.98, f32[64,64]{1,0:T(8,128)S(1)} %copy-done.33, f32[64,64]{1,0:T(8,128)S(1)} %copy-done.32, ...), kind=kOutput, calls=%fused_computation.82 | convolution fusion | flops 53215232 | bytes 622848 | tf_op jit(solution)/shard_map/nij,knj->kni/dot_general | solution.py:102
  66.7 6.1 %fusion.48 = f32[64,16,64]{2,1,0:T(8,128)S(1)} fusion(f32[64]{0:T(128)S(1)} %get-tuple-element.147, f32[64,64]{1,0:T(8,128)S(1)} %get-tuple-element.103, f32[64,64]{1,0:T(8,128)S(1)} %get-tuple-element.99, f32[64,64]{1,0:T(8,128)S(1)} %get-tuple-element.88, f32[64,64]{1,0:T(8,128)S(1)} %copy-done.33, f32[64,64]{1,0:T(8,128)S(1)} %copy-done.32, ...), kind=kOutput, calls=%fused_computation.56 | convolution fusion | flops 53215232 | bytes 622848 | tf_op jit(solution)/shard_map/nij,knj->kni/dot_general | solution.py:102
  72.7 6.1 %fusion.138 = f32[64,16,64]{2,1,0:T(8,128)S(1)} fusion(f32[64,16,64]{2,1,0:T(8,128)S(1)} %fusion.74, f32[64,16,64]{2,1,0:T(8,128)S(1)} %fusion.87, f32[64]{0:T(128)S(1)} %get-tuple-element.146, f32[64,64]{1,0:T(8,128)S(1)} %get-tuple-element.104, f32[64,64]{1,0:T(8,128)S(1)} %copy-done.33, f32[64,64]{1,0:T(8,128)S(1)} %get-tuple-element.112, ...), kind=kOutput, calls=%fused_computation.143 | convolution fusion | flops 53346304 | bytes 1147136 | tf_op jit(solution)/shard_map/nij,knj->kni/dot_general | solution.py:102
  78.9 6.0 %fusion.144 = f32[64,16,64]{2,1,0:T(8,128)} fusion(f32[64,16,64]{2,1,0:T(8,128)S(1)} %fusion.48, f32[64,16,64]{2,1,0:T(8,128)S(1)} %fusion.138, f32[64]{0:T(128)S(1)} %get-tuple-element.143, f32[64,64]{1,0:T(8,128)S(1)} %get-tuple-element.86, f32[64,64]{1,0:T(8,128)S(1)} %get-tuple-element.87, f32[64,64]{1,0:T(8,128)S(1)} %get-tuple-element.85, ...), kind=kOutput, calls=%fused_computation.145 | convolution fusion | flops 53346304 | bytes 1147136 | tf_op jit(solution)/shard_map/nij,knj->kni/dot_general | solution.py:102
  85.6 1.7 collective-permute-start.6
  88.1 4.3 %gather_fusion.1 = f32[1280,3,32]{2,1,0:T(4,128)S(1)} fusion(f32[3,32,86]{1,0,2:T(4,128)S(1)} %copy.122, s32[2048]{0:T(1024)S(1)} %pad_clamp_fusion), kind=kCustom, calls=%fused_computation.1 | custom fusion | bytes 988160 | tf_op jit(solution)/shard_map/while/body/eval_jaxpr/jit(_take)/gather | solution.py:77
  92.5 2.5 %copy.152 = f32[20,64,3,32]{1,0,3,2:T(8,128)} copy(f32[20,64,3,32]{3,2,1,0:T(4,128)S(1)} %bitcast.210) | data formatting | bytes 983040 | tf_op jit(solution)/shard_map/while/body/eval_jaxpr/jit(_take)/gather | solution.py:77
  99.9 1.8 collective-permute-start.7
  102.4 5.5 %gather_fusion = f32[1280,32,16]{1,2,0:T(8,128)} fusion(f32[32,16,86]{0,1,2:T(8,128)S(1)} %copy.120, s32[2048]{0:T(1024)S(1)} %pad_clamp_fusion), kind=kCustom, calls=%fused_computation | custom fusion | bytes 5248000 | tf_op jit(solution)/shard_map/while/body/eval_jaxpr/jit(_take)/gather | solution.py:76
  109.0 31.4 %fusion.130 = f32[64,16,32]{2,1,0:T(8,128)} fusion(f32[20,64]{1,0:T(8,128)S(1)} %copy-done.41, f32[32,20,64]{0,2,1:T(8,128)} %copy.128, f32[32,64]{0,1:T(8,128)S(1)} %copy-done.30, f32[32,20,64]{0,2,1:T(8,128)S(1)} %copy-done.15, f32[32,64]{0,1:T(8,128)S(1)} %copy-done.29, f32[32,20,64]{0,2,1:T(8,128)S(1)} %copy.124, f32[32,64]{0,1:T(8,128)S(1)} %copy-done.28, ...), kind=kOutput, calls=%fused_computation.141 | convolution fusion | flops 266731520 | bytes 3275008 | tf_op jit(solution)/shard_map/while/body/eval_jaxpr/absn,bksn->akn/dot_general | solution.py:81
  141.8 1.9 reshape.373
  149.0 1.7 copy.136
  152.4 2.2 %gather_fusion.3 = f32[320,3,32]{2,1,0:T(4,128)S(1)} fusion(f32[3,32,512]{1,0,2:T(4,128)S(1)} %copy.137, s32[1024]{0:T(1024)S(1)} %copy-done.22), kind=kCustom, calls=%fused_computation.3 | custom fusion | bytes 247040 | tf_op jit(solution)/shard_map/while/body/eval_jaxpr/jit(_take)/gather | solution.py:77
  160.2 4.6 %slice.466 = f32[32,16,32,16]{0,1,3,2:T(8,128)} slice(f32[32,16,32,21]{0,1,3,2:T(8,128)} %bitcast.213), slice={[0:32], [0:16], [0:32], [5:21]} | slice | bytes 2097152 | tf_op jit(solution)/shard_map/slice | solution.py:145
  166.2 3.0 %gather_fusion.2 = f32[320,32,16]{1,2,0:T(8,128)S(1)} fusion(f32[32,16,512]{0,1,2:T(8,128)} %bitcast.200, s32[1024]{0:T(1024)S(1)} %copy-done.22), kind=kCustom, calls=%fused_computation.2 | custom fusion | bytes 1312000 | tf_op jit(solution)/shard_map/while/body/eval_jaxpr/jit(_take)/gather | solution.py:76
  169.4 3.2 %fusion.153 = f32[4,16,32]{2,1,0:T(8,128)S(1)} fusion(f32[20,4,32,16]{2,3,1,0:T(8,128)S(1)} %bitcast.198, f32[20,4]{1,0:T(8,128)} %get-tuple-element.139, f32[32,20,4]{0,2,1:T(4,128)} %get-tuple-element.124, f32[32,4]{0,1:T(4,128)} %bitcast.236, f32[32,20,4]{0,2,1:T(4,128)} %get-tuple-element.125, f32[32,4]{0,1:T(4,128)} %bitcast.235, ...), kind=kOutput, calls=%fused_computation.150 | convolution fusion | flops 16670720 | bytes 204688 | tf_op jit(solution)/shard_map/while/body/eval_jaxpr/absn,bksn->akn/dot_general | solution.py:81
  173.8 8.3 %fusion.148 = f32[16,16,32]{2,1,0:T(8,128)S(1)} fusion(f32[20,16]{1,0:T(8,128)S(1)} %copy-done.40, f32[32,20,16]{0,2,1:T(8,128)S(1)} %copy-done.26, f32[32,16]{0,1:T(8,128)S(1)} %copy-done.44, f32[32,20,16]{0,2,1:T(8,128)S(1)} %copy-done.27, f32[32,16]{0,1:T(8,128)S(1)} %copy-done.43, f32[32,20,16]{0,2,1:T(8,128)S(1)} %copy-done.25, ...), kind=kOutput, calls=%fused_computation.149 | convolution fusion | flops 66682880 | bytes 818752 | tf_op jit(solution)/shard_map/while/body/eval_jaxpr/absn,bksn->akn/dot_general | solution.py:81
  182.7 1.7 fusion.129
  (219 shorter events, 55.3 us)
Async XLA Ops:
  6.5 9.7 %copy-start.18 = (f32[32,4096]{1,0:T(8,128)S(1)}, f32[32,4096]{1,0:T(8,128)}, u32[]{:S(2)}) copy-start(f32[32,4096]{1,0:T(8,128)} %param.10) | copy-start | bytes 1572868
  6.5 10.1 %copy-start.11 = (f32[16,4096]{1,0:T(8,128)S(1)}, f32[16,4096]{1,0:T(8,128)}, u32[]{:S(2)}) copy-start(f32[16,4096]{1,0:T(8,128)} %param.9) | copy-start | bytes 786436
  6.5 151.3 %all-gather.2.cloned.1.call-start = ((), (), s32[]{:S(2)}) async-start(), calls=%async_computation | async-start | bytes 5677056 | tf_op jit(solution)/shard_map/all_gather | solution.py:133
  6.5 41.9 %collective-permute-start.4 = (f32[3,32,21]{2,1,0:T(8,128)}, f32[3,32,21]{2,1,0:T(8,128)S(1)}, u32[]{:S(2)}, u32[]{:S(2)}) collective-permute-start(f32[3,32,21]{2,1,0:T(8,128)} %bitcast.203), channel_id=1, source_target_pairs={{0,31},{1,0},{2,1},{3,2},{4,3},{5,4},{6,5},{7,6},{8,7},{9,8},{10,9... | collective-permute-start | bytes 24200 | tf_op jit(solution)/shard_map/ppermute | solution.py:23
  16.7 7.7 %copy-start = (f32[32,64,64]{2,1,0:T(8,128)}, f32[32,64,64]{2,1,0:T(8,128)S(1)}, u32[]{:S(2)}) copy-start(f32[32,64,64]{2,1,0:T(8,128)S(1)} %reshape.364) | copy-start | bytes 1572868
  18.8 6.7 %copy-start.2 = (f32[32,32,64]{1,0,2:T(8,128)}, f32[32,32,64]{1,0,2:T(8,128)S(1)}, u32[]{:S(2)}) copy-start(f32[32,32,64]{1,0,2:T(8,128)S(1)} %copy.162) | copy-start | bytes 786436
  25.5 9.7 %copy-start.21 = (s32[84,20]{0,1:T(8,128)S(1)}, s32[84,20]{0,1:T(8,128)}, u32[]{:S(2)}) copy-start(s32[84,20]{0,1:T(8,128)} %param.14) | copy-start | bytes 20164
  25.5 10.5 %copy-start.52 = (s32[1,32]{1,0:T(1,128)S(1)}, s32[1,32]{1,0:T(1,128)}, u32[]{:S(2)}) copy-start(s32[1,32]{1,0:T(1,128)} %param.15) | copy-start | bytes 388
  25.5 13.7 %copy-start.46 = (s32[64,5]{0,1:T(8,128)S(1)}, s32[64,5]{0,1:T(8,128)}, u32[]{:S(2)}) copy-start(s32[64,5]{0,1:T(8,128)} %param.13) | copy-start | bytes 3844
  27.3 60.0 %copy-start.13 = (f32[3,32,64]{2,1,0:T(8,128)}, f32[3,32,64]{2,1,0:T(8,128)S(1)}, u32[]{:S(2)}) copy-start(f32[3,32,64]{2,1,0:T(8,128)S(1)} %slice.381) | copy-start | bytes 73732
  28.2 59.0 %collective-permute-start.2 = (f32[608,11]{1,0:T(8,128)}, f32[608,11]{1,0:T(8,128)S(1)}, u32[]{:S(2)}, u32[]{:S(2)}) collective-permute-start(f32[608,11]{1,0:T(8,128)} %get-tuple-element.121), channel_id=1, source_target_pairs={{0,1},{1,2},{2,3},{3,4},{4,5},{5,6},{6,7},{7,8},{8,9},{9,10},{10,1... | collective-permute-start | bytes 80264 | tf_op jit(solution)/shard_map/ppermute | solution.py:43
  29.5 57.7 %collective-permute-start.3 = (f32[608,11]{1,0:T(8,128)}, f32[608,11]{1,0:T(8,128)S(1)}, u32[]{:S(2)}, u32[]{:S(2)}) collective-permute-start(f32[608,11]{1,0:T(8,128)} %get-tuple-element.122), channel_id=1, source_target_pairs={{1,0},{2,1},{3,2},{4,3},{5,4},{6,5},{7,6},{8,7},{9,8},{10,9},{11,1... | collective-permute-start | bytes 80264 | tf_op jit(solution)/shard_map/ppermute | solution.py:45
  30.9 22.6 %collective-permute-start = (f32[19,128]{1,0:T(8,128)S(1)}, f32[19,128]{1,0:T(8,128)S(1)}, u32[]{:S(2)}, u32[]{:S(2)}) collective-permute-start(f32[19,128]{1,0:T(8,128)S(1)} %get-tuple-element.119), channel_id=1, source_target_pairs={{0,1},{1,2},{2,3},{3,4},{4,5},{5,6},{6,7},{7,8},{8,9},{9,10},{10,1... | collective-permute-start | bytes 29192 | tf_op jit(solution)/shard_map/ppermute | solution.py:43
  33.9 19.5 %collective-permute-start.1 = (f32[19,128]{1,0:T(8,128)S(1)}, f32[19,128]{1,0:T(8,128)S(1)}, u32[]{:S(2)}, u32[]{:S(2)}) collective-permute-start(f32[19,128]{1,0:T(8,128)S(1)} %get-tuple-element.120), channel_id=1, source_target_pairs={{1,0},{2,1},{3,2},{4,3},{5,4},{6,5},{7,6},{8,7},{9,8},{10,9},{11,1... | collective-permute-start | bytes 29192 | tf_op jit(solution)/shard_map/ppermute | solution.py:45
  48.6 36.3 %collective-permute-start.5 = (f32[3,32,42]{2,1,0:T(8,128)S(1)}, f32[3,32,42]{2,1,0:T(8,128)S(1)}, u32[]{:S(2)}, u32[]{:S(2)}) collective-permute-start(f32[3,32,42]{2,1,0:T(8,128)S(1)} %pad_maximum_fusion.6), channel_id=1, source_target_pairs={{0,30},{1,31},{2,0},{3,1},{4,2},{5,3},{6,4},{7,5},{8,6},{9,7},{10,... | collective-permute-start | bytes 48392 | tf_op jit(solution)/shard_map/ppermute | solution.py:23
  85.6 13.4 %collective-permute-start.6 = (f32[3,32,84]{2,1,0:T(8,128)}, f32[3,32,84]{2,1,0:T(8,128)}, u32[]{:S(2)}, u32[]{:S(2)}) collective-permute-start(f32[3,32,84]{2,1,0:T(8,128)} %pad_maximum_fusion.7), channel_id=1, source_target_pairs={{0,28},{1,29},{2,30},{3,31},{4,0},{5,1},{6,2},{7,3},{8,4},{9,5},{1... | collective-permute-start | bytes 96776 | tf_op jit(solution)/shard_map/ppermute | solution.py:23
  99.9 8.0 %collective-permute-start.7 = (f32[3,32,168]{2,1,0:T(8,128)S(1)}, f32[3,32,168]{2,1,0:T(8,128)S(1)}, u32[]{:S(2)}, u32[]{:S(2)}) collective-permute-start(f32[3,32,168]{2,1,0:T(8,128)S(1)} %pad_maximum_fusion.4), channel_id=1, source_target_pairs={{0,24},{1,25},{2,26},{3,27},{4,28},{5,29},{6,30},{7,31},{8,0},{9,1... | collective-permute-start | bytes 193544 | tf_op jit(solution)/shard_map/ppermute | solution.py:23
  102.4 6.6 %copy-start.28 = (f32[32,64]{0,1:T(8,128)S(1)}, f32[32,64]{0,1:T(8,128)}, u32[]{:S(2)}) copy-start(f32[32,64]{0,1:T(8,128)} %copy.121) | copy-start | bytes 24580
  102.4 6.6 %copy-start.29 = (f32[32,64]{0,1:T(8,128)S(1)}, f32[32,64]{0,1:T(8,128)}, u32[]{:S(2)}) copy-start(f32[32,64]{0,1:T(8,128)} %copy.125) | copy-start | bytes 24580
  102.4 6.6 %copy-start.30 = (f32[32,64]{0,1:T(8,128)S(1)}, f32[32,64]{0,1:T(8,128)}, u32[]{:S(2)}) copy-start(f32[32,64]{0,1:T(8,128)} %copy.127) | copy-start | bytes 24580
  108.9 31.5 %collective-permute-start.8 = (f32[3,32,336]{2,1,0:T(8,128)S(1)}, f32[3,32,336]{2,1,0:T(8,128)S(1)}, u32[]{:S(2)}, u32[]{:S(2)}) collective-permute-start(f32[3,32,336]{2,1,0:T(8,128)S(1)} %concatenate.53), channel_id=1, source_target_pairs={{0,16},{1,17},{2,18},{3,19},{4,20},{5,21},{6,22},{7,23},{8,24},{9,... | collective-permute-start | bytes 387080 | tf_op jit(solution)/shard_map/ppermute | solution.py:23
  173.7 8.4 %copy-start.8 = (f32[32,32,16]{1,0,2:T(8,128)S(1)}, f32[32,32,16]{1,0,2:T(8,128)}, u32[]{:S(2)}) copy-start(f32[32,32,16]{1,0,2:T(8,128)} %copy-done.7) | copy-start | bytes 196612
  173.8 8.9 %copy-start.3 = (f32[32,32,64]{1,0,2:T(8,128)S(1)}, f32[32,32,64]{1,0,2:T(8,128)}, u32[]{:S(2)}) copy-start(f32[32,32,64]{1,0,2:T(8,128)} %copy-done.2) | copy-start | bytes 786436
  173.8 8.9 %copy-start.20 = (f32[64,16,32]{2,1,0:T(8,128)S(1)}, f32[64,16,32]{2,1,0:T(8,128)}, u32[]{:S(2)}) copy-start(f32[64,16,32]{2,1,0:T(8,128)} %fusion.130) | copy-start | bytes 393220
  (40 other events, 145.2 us)
Sparse Core Ops, SparseCore 0:
  27.0 65.0 all-gather.1
